TPU v7x, 256 devices: a whole 4x4x8 slice. The times are simulated.
256 devices in a mesh: dp: 4 (over y), seq: 16 (over z, core), mp: 4 (over x).
Axes of the slice: x: 4, y: 4, z: 8, core: 2. Of those that a mesh axis runs over, the one named last changes fastest.
Arguments:
- q_self: bfloat16 [4, 1024, 4096], P('dp', 'seq', 'mp'), may hold values from -12 to 12
- k_self: bfloat16 [4, 1024, 4096], P('dp', 'seq', 'mp'), may hold values from -3 to 3
- v_self: bfloat16 [4, 1024, 4096], P('dp', 'seq', 'mp'), may hold values from -0.75 to 0.75
- out_grad_self: bfloat16 [4, 1024, 4096], P('dp', 'seq', 'mp'), may hold values from -6 to 6
- q_cross: bfloat16 [4, 1024, 4096], P('dp', 'seq', 'mp'), may hold values from -12 to 12
- k_cross: bfloat16 [4, 2048, 4096], P('dp', 'seq', 'mp'), may hold values from -3 to 3
- v_cross: bfloat16 [4, 2048, 4096], P('dp', 'seq', 'mp'), may hold values from -0.75 to 0.75
- out_grad_cross: bfloat16 [4, 1024, 4096], P('dp', 'seq', 'mp'), may hold values from -8 to 8
- dec_lengths: int32 [4, 16], P('dp'), may hold values from 1 to 640, as said below
- enc_lengths: int32 [4, 16], P('dp'), may hold values from 1 to 1280, as said below
- rel_bias: float32 [32, 64], P(None, 'mp'), may hold values from -4 to 4
Outputs:
- grad_q_self: bfloat16 [4, 1024, 4096], P('dp', 'seq', 'mp')
- grad_k_self: bfloat16 [4, 1024, 4096], P('dp', 'seq', 'mp')
- grad_v_self: bfloat16 [4, 1024, 4096], P('dp', 'seq', 'mp')
- grad_q_cross: bfloat16 [4, 1024, 4096], P('dp', 'seq', 'mp')
- grad_k_cross: bfloat16 [4, 2048, 4096], P('dp', 'seq', 'mp')
- grad_v_cross: bfloat16 [4, 2048, 4096], P('dp', 'seq', 'mp')
- bias_grad: float32 [32, 64], P(None, 'mp')
Inputs may be any that keep to these rules, and one draw needn't show every extreme that they name: `dec_lengths`: row p lists the decoder lengths of the 16 examples of pack p in order; they sum to 1024 and the largest is exactly 640. `enc_lengths`: row p lists the encoder lengths of the same 16 examples in the same order; they sum to 2048. The example with 640 decoder rows has exactly 1280 encoder rows; every other example has at least as many encoder rows as decoder rows and at most three times as many.
All inputs are finite; a program needn't handle non-finite values.
Results may differ from a plain program's by a relative error of at most 0.039.
Values may be sent and summed in bfloat16 or wider, within the bound.
A program may use at most 128 MiB of HBM per device.

v0:
```python
import math
import jax
import jax.numpy as jnp
from jax import lax
from jax.sharding import PartitionSpec as P

HEAD_DIM = 64
BUCKETS = 32
DISTANCE = 128


def bucket_of(distances):
    exact_count = BUCKETS // 2
    bucketed = jnp.full(distances.shape, exact_count, jnp.int32)
    for level_index in range(1, BUCKETS - exact_count):
        threshold = math.ceil(
            exact_count * (DISTANCE / exact_count) ** (level_index / (BUCKETS - exact_count))
        )
        bucketed = bucketed + (distances >= threshold).astype(jnp.int32)
    return jnp.where(distances < exact_count, distances, bucketed)


def example_ids(total_rows, lengths):
    segment_ends = jnp.cumsum(lengths)
    positions = jnp.arange(total_rows, dtype=jnp.int32)
    return jnp.sum((positions[:, None] >= segment_ends[None, :]).astype(jnp.int32), axis=1)


def distance_table(rel_bias, offset_base, table_span):
    distances = offset_base + jnp.arange(table_span, dtype=jnp.int32)
    buckets = bucket_of(jnp.maximum(distances, 0))
    one_hot = (buckets[None, :] == jnp.arange(rel_bias.shape[0], dtype=jnp.int32)[:, None]).astype(
        jnp.float32
    )
    bias_table = jnp.einsum("bh,bl->hl", rel_bias, one_hot, precision=lax.Precision.HIGHEST)
    return (one_hot, bias_table)


def spread(bias_table, row_count, col_count):
    full_span = row_count + col_count - 1
    leading = bias_table.shape[:-1]
    tiled_rows = jnp.broadcast_to(bias_table[..., None, :], leading + (row_count, full_span))
    flat_rows = tiled_rows.reshape(leading + (row_count * full_span,))
    flat_rows = jnp.pad(flat_rows, [(0, 0)] * len(leading) + [(0, row_count)])
    skewed = flat_rows.reshape(leading + (row_count, full_span + 1))[..., :col_count]
    return skewed[..., ::-1]


def collapse(matrix, row_count, col_count):
    full_span = row_count + col_count - 1
    leading = matrix.shape[:-2]
    flipped = matrix[..., ::-1]
    padded = jnp.pad(flipped, [(0, 0)] * len(leading) + [(0, 0), (0, row_count)])
    flat_rows = padded.reshape(leading + (row_count * (full_span + 1),))[
        ..., : row_count * full_span
    ]
    return jnp.sum(flat_rows.reshape(leading + (row_count, full_span)), axis=-2)


def shard_group(shard_count, row_count):
    group_size = 1
    while group_size < shard_count and (
        shard_count % group_size != 0 or group_size * row_count < 384
    ):
        group_size += 1
    return group_size


def query_side(
    queries,
    out_grads,
    all_keys,
    all_values,
    key_ids,
    query_ids,
    query_start,
    rel_bias,
    block_rows,
    causal,
):
    row_count, head_count, head_size = queries.shape
    block_count = all_keys.shape[0] // block_rows
    query_pos = query_start + jnp.arange(row_count, dtype=jnp.int32)
    block_ids = jnp.arange(block_count, dtype=jnp.int32)

    def scores_of(block_id):
        key_first = block_id * block_rows
        key_block = lax.dynamic_slice_in_dim(all_keys, key_first, block_rows, 0)
        key_block_ids = lax.dynamic_slice_in_dim(key_ids, key_first, block_rows, 0)
        scores = jnp.einsum("thd,uhd->htu", queries, key_block, preferred_element_type=jnp.float32)
        allowed = query_ids[:, None] == key_block_ids[None, :]
        one_hot = jnp.zeros((1, 1), jnp.float32)
        if causal:
            key_pos = key_first + jnp.arange(block_rows, dtype=jnp.int32)
            allowed = allowed & (query_pos[:, None] >= key_pos[None, :])
            one_hot, bias_table = distance_table(
                rel_bias, query_start - key_first - (block_rows - 1), row_count + block_rows - 1
            )
            scores = scores + spread(bias_table, row_count, block_rows)
        return (jnp.where(allowed[None], scores, -1e30), one_hot)

    def stat_step(running, block_id):
        row_high, total_sum = running
        scores, unused_hot = scores_of(block_id)
        new_high = jnp.maximum(row_high, jnp.max(scores, axis=2))
        total_sum = total_sum * jnp.exp(row_high - new_high) + jnp.sum(
            jnp.exp(scores - new_high[:, :, None]), axis=2
        )
        return ((new_high, total_sum), None)

    start_state = (
        jnp.full((head_count, row_count), -1e30, jnp.float32),
        jnp.zeros((head_count, row_count), jnp.float32),
    )
    (row_high, total_sum), unused_stats = lax.scan(stat_step, start_state, block_ids)

    def weights_of(scores):
        return jnp.exp(scores - row_high[:, :, None]) / total_sum[:, :, None]

    def out_step(summed, block_id):
        scores, unused_hot = scores_of(block_id)
        narrow_weights = weights_of(scores).astype(jnp.bfloat16)
        value_block = lax.dynamic_slice_in_dim(all_values, block_id * block_rows, block_rows, 0)
        return (
            summed
            + jnp.einsum(
                "htu,uhd->thd", narrow_weights, value_block, preferred_element_type=jnp.float32
            ),
            None,
        )

    summed, unused_outs = lax.scan(
        out_step, jnp.zeros((row_count, head_count, head_size), jnp.float32), block_ids
    )
    outputs = summed.astype(jnp.bfloat16)
    row_delta = jnp.einsum("thd,thd->ht", out_grads, outputs, preferred_element_type=jnp.float32)

    def grad_step(running, block_id):
        query_grad, bias_grad_sum = running
        scores, one_hot = scores_of(block_id)
        weights = weights_of(scores)
        narrow_weights = weights.astype(jnp.bfloat16)
        key_block = lax.dynamic_slice_in_dim(all_keys, block_id * block_rows, block_rows, 0)
        value_block = lax.dynamic_slice_in_dim(all_values, block_id * block_rows, block_rows, 0)
        weight_grads = jnp.einsum(
            "thd,uhd->htu", out_grads, value_block, preferred_element_type=jnp.float32
        )
        score_grads = weights * (weight_grads - row_delta[:, :, None])
        narrow_grads = score_grads.astype(jnp.bfloat16)
        query_grad = query_grad + jnp.einsum(
            "htu,uhd->thd", narrow_grads, key_block, preferred_element_type=jnp.float32
        )
        if causal:
            bias_grad_sum = bias_grad_sum + jnp.einsum(
                "hl,bl->bh",
                collapse(score_grads, row_count, block_rows),
                one_hot,
                precision=lax.Precision.HIGHEST,
            )
        key_term = jnp.einsum(
            "htu,thd->uhd", narrow_grads, queries, preferred_element_type=jnp.float32
        )
        value_term = jnp.einsum(
            "htu,thd->uhd", narrow_weights, out_grads, preferred_element_type=jnp.float32
        )
        grad_term = jnp.concatenate(
            [
                key_term.reshape(block_rows, head_count * head_size),
                value_term.reshape(block_rows, head_count * head_size),
            ],
            axis=1,
        ).astype(jnp.bfloat16)
        return ((query_grad, bias_grad_sum), grad_term)

    grad_state = (
        jnp.zeros((row_count, head_count, head_size), jnp.float32),
        jnp.zeros((rel_bias.shape[0], head_count), jnp.float32),
    )
    (query_grad, bias_grad_sum), grad_terms = lax.scan(grad_step, grad_state, block_ids)
    grad_terms = grad_terms.reshape(block_count * block_rows, 2 * head_count * head_size)
    query_grad = query_grad.astype(jnp.bfloat16).reshape(row_count, head_count * head_size)
    return (query_grad, grad_terms, bias_grad_sum, (row_high, total_sum, row_delta))


def on_device(
    q_self,
    k_self,
    v_self,
    out_grad_self,
    q_cross,
    k_cross,
    v_cross,
    out_grad_cross,
    dec_lengths,
    enc_lengths,
    rel_bias,
):
    seq_count = lax.axis_size("seq")
    seq_place = lax.axis_index("seq")
    dec_rows = q_self.shape[1]
    enc_rows = k_cross.shape[1]
    feature_count = q_self.shape[2]
    head_count = feature_count // HEAD_DIM
    dec_total = dec_rows * seq_count
    enc_total = enc_rows * seq_count
    dec_start = seq_place * dec_rows
    dec_ids = example_ids(dec_total, dec_lengths[0])
    enc_ids = example_ids(enc_total, enc_lengths[0])
    my_dec_ids = lax.dynamic_slice_in_dim(dec_ids, dec_start, dec_rows, 0)

    def split_heads(tensor):
        return tensor.reshape(tensor.shape[0] * tensor.shape[1], head_count, HEAD_DIM)

    gathered = (
        lax.all_gather(k_self, "seq", axis=1, tiled=True),
        lax.all_gather(v_self, "seq", axis=1, tiled=True),
        lax.all_gather(k_cross, "seq", axis=1, tiled=True),
        lax.all_gather(v_cross, "seq", axis=1, tiled=True),
    )
    self_group = shard_group(seq_count, dec_rows)
    cross_group = shard_group(seq_count, enc_rows)
    self_dq, self_terms, self_bias, self_stats = query_side(
        split_heads(q_self),
        split_heads(out_grad_self),
        split_heads(gathered[0]),
        split_heads(gathered[1]),
        dec_ids,
        my_dec_ids,
        dec_start,
        rel_bias,
        self_group * dec_rows,
        True,
    )
    cross_dq, cross_terms, unused_bias, cross_stats = query_side(
        split_heads(q_cross),
        split_heads(out_grad_cross),
        split_heads(gathered[2]),
        split_heads(gathered[3]),
        enc_ids,
        my_dec_ids,
        dec_start,
        rel_bias,
        cross_group * enc_rows,
        False,
    )
    self_sums = lax.psum_scatter(
        self_terms.astype(jnp.float32).astype(jnp.bfloat16), "seq", scatter_dimension=0, tiled=True
    ).astype(jnp.float32)
    cross_sums = lax.psum_scatter(
        cross_terms.astype(jnp.float32).astype(jnp.bfloat16), "seq", scatter_dimension=0, tiled=True
    ).astype(jnp.float32)
    self_key_grad = self_sums[:, :feature_count]
    self_value_grad = self_sums[:, feature_count:]
    cross_key_grad = cross_sums[:, :feature_count]
    cross_value_grad = cross_sums[:, feature_count:]
    bias_total = lax.psum(self_bias, ("dp", "seq"))
    bias_grad = bias_total * (1.0 / math.sqrt(lax.axis_size("dp") * dec_total))
    return (
        self_dq.reshape(1, dec_rows, feature_count),
        self_key_grad.reshape(1, dec_rows, feature_count).astype(jnp.bfloat16),
        self_value_grad.reshape(1, dec_rows, feature_count).astype(jnp.bfloat16),
        cross_dq.reshape(1, dec_rows, feature_count),
        cross_key_grad.reshape(1, enc_rows, feature_count).astype(jnp.bfloat16),
        cross_value_grad.reshape(1, enc_rows, feature_count).astype(jnp.bfloat16),
        bias_grad,
    )


def solution(mesh):
    return jax.shard_map(
        on_device,
        mesh=mesh,
        in_specs=(
            P("dp", "seq", "mp"),
            P("dp", "seq", "mp"),
            P("dp", "seq", "mp"),
            P("dp", "seq", "mp"),
            P("dp", "seq", "mp"),
            P("dp", "seq", "mp"),
            P("dp", "seq", "mp"),
            P("dp", "seq", "mp"),
            P("dp", None),
            P("dp", None),
            P(None, "mp"),
        ),
        out_specs=(
            P("dp", "seq", "mp"),
            P("dp", "seq", "mp"),
            P("dp", "seq", "mp"),
            P("dp", "seq", "mp"),
            P("dp", "seq", "mp"),
            P("dp", "seq", "mp"),
            P(None, "mp"),
        ),
        check_vma=False,
    )
```

profile of v0, /device:TPU:2, one launch (start us, length us, event | category | flops | bytes accessed | tf_op | source)
XLA Modules:
  0.0 455.4 jit_solution(5825784003897655049)
XLA Ops:
  17.9 34.6 %all-gather.5.cloned.1.call-done = bf16[1,1024,1024]{2,1,0:T(8,128)(2,1)} async-done(((bf16[1,64,1024]{2,1,0:T(8,128)(2,1)}), bf16[1,1024,1024]{2,1,0:T(8,128)(2,1)}) %all-gather.5.cloned.1.call-update) | async-done | bytes 2097168 | tf_op jit(solution)/shard_map/all_gather | solution.py:215
  52.6 3.9 copy.70
  56.5 31.9 %while.91 = (s32[]{:T(128)}, f32[16,64]{1,0:T(8,128)S(1)}, f32[16,64]{1,0:T(8,128)S(1)}, s32[64]{0:T(128)S(1)}, s32[2]{0:T(128)S(1)}, /*index=5*/s32[1024]{0:T(1...) while((s32[]{:T(128)}, f32[16,64]{1,0:T(8,128)S(1)}, ...), condition=%wide.region_5.6_spmd.clone.clone.clone, body=%wide.region_2.0_spmd.clone.clone.clone.sunk | while | flops 73413688 | bytes 34665884 | solution.py:115
  88.4 4.1 all-gather.7.cloned.1.call-done
  92.5 3.9 copy.74
  96.4 34.2 %while.92 = (s32[]{:T(128)}, f32[64,16,64]{0,2,1:T(8,128)}, s32[2]{0:T(128)S(1)}, bf16[1024,16,64]{0,2,1:T(8,128)(2,1)}, s32[64]{0:T(128)S(1)}, /*index=5*/s32[1...) while((s32[]{:T(128)}, f32[64,16,64]{0,2,1:T(8,128)}, ...), condition=%wide.region_7.8_spmd.clone.clone.clone, body=%wide.region_6.7_spmd.clone.clone.clone.sunk | while | flops 140648496 | bytes 34098144 | solution.py:132
  109.2 3.4 fusion.213
  126.3 3.4 fusion.213
  131.7 80.7 %while.93 = (s32[]{:T(128)}, f32[64,16,64]{0,2,1:T(8,128)}, f32[32,16]{0,1:T(8,128)S(1)}, bf16[2,512,2048]{2,1,0:T(8,128)(2,1)}, s32[2]{0:T(128)S(1)}, /*index=5...) while((s32[]{:T(128)}, f32[64,16,64]{0,2,1:T(8,128)}, ...), condition=%wide.region_10.11_spmd.clone.clone.clone, body=%wide.region_8.10_spmd.clone.clone.clone.sunk | while | flops 353446976 | bytes 101543680 | solution.py:179
  164.8 3.7 reshape.726
  168.9 3.3 constant_dynamic-update-slice_fusion.5
  184.9 2.7 fusion.226
  205.1 3.7 reshape.726
  209.2 3.3 constant_dynamic-update-slice_fusion.5
  212.6 6.7 %copy.79 = bf16[1,2048,1024]{1,2,0:T(8,128)(2,1)} copy(bf16[1,2048,1024]{2,1,0:T(8,128)(2,1)} %all-gather.9.cloned.1.call-done) | data formatting | bytes 8388608 | tf_op jit(solution)/shard_map/all_gather | solution.py:217
  219.4 15.2 %while.88 = (s32[]{:T(128)}, f32[16,64]{1,0:T(8,128)S(1)}, f32[16,64]{1,0:T(8,128)S(1)}, s32[64]{0:T(128)S(1)}, s32[4]{0:T(128)S(1)}, /*index=5*/s32[2048]{0:T(1...) while((s32[]{:T(128)}, f32[16,64]{1,0:T(8,128)S(1)}, ...), condition=%wide.region_17.18_spmd.clone, body=%wide.region_14.17_spmd.clone.sunk | while | flops 69768200 | bytes 5532106 | solution.py:115
  234.6 6.6 %copy.83 = bf16[1,2048,1024]{1,2,0:T(8,128)(2,1)} copy(bf16[1,2048,1024]{2,1,0:T(8,128)(2,1)} %all-gather.11.cloned.1.call-done) | data formatting | bytes 8388608 | tf_op jit(solution)/shard_map/all_gather | solution.py:218
  241.3 16.1 %while.89 = (s32[]{:T(128)}, f32[64,16,64]{0,2,1:T(8,128)S(1)}, s32[4]{0:T(128)S(1)}, bf16[2048,16,64]{0,2,1:T(8,128)(2,1)}, s32[64]{0:T(128)S(1)}, /*index=5*/s...) while((s32[]{:T(128)}, f32[64,16,64]{0,2,1:T(8,128)S(1)}, ...), condition=%wide.region_19.20_spmd.clone, body=%wide.region_18.19_spmd.clone.sunk | while | flops 136478720 | bytes 2834388 | solution.py:132
  257.5 54.1 %while.90 = (s32[]{:T(128)}, f32[64,16,64]{0,2,1:T(8,128)S(1)}, bf16[4,512,2048]{2,1,0:T(8,128)(2,1)}, s32[4]{0:T(128)S(1)}, bf16[2048,16,64]{0,2,1:T(8,128)(2,1...) while((s32[]{:T(128)}, f32[64,16,64]{0,2,1:T(8,128)S(1)}, ...), condition=%wide.region_21.22_spmd.clone, body=%wide.region_20.21_spmd.clone.sunk | while | flops 344621056 | bytes 28396028 | solution.py:179
  266.6 2.9 copy.116
  280.2 2.9 copy.116
  293.6 2.9 copy.116
  307.1 2.9 copy.116
  313.4 130.1 %psum.7 = f32[32,16]{0,1:T(8,128)S(1)} all-reduce(f32[32,16]{0,1:T(8,128)S(1)} %get-tuple-element.693), channel_id=1, replica_groups=mesh['dp'=4,'seq'=16,'mp'=4] {'dp','seq'}, use_global_device_ids=true, to_apply=%region_23.24 | all-reduce | flops 512 | bytes 4096 | tf_op jit(solution)/shard_map/psum | solution.py:256
  (318 shorter events, 202.3 us)
Async XLA Ops:
  7.2 9.6 %copy-start.19 = (bf16[1,64,1024]{2,1,0:T(8,128)(2,1)S(1)}, bf16[1,64,1024]{2,1,0:T(8,128)(2,1)}, u32[]{:S(2)}) copy-start(bf16[1,64,1024]{2,1,0:T(8,128)(2,1)} %param.27) | copy-start | bytes 393220
  7.2 45.4 %all-gather.5.cloned.1.call-start = ((), (), s32[]{:S(2)}) async-start(), calls=%async_computation.2 | async-start | bytes 2228224 | tf_op jit(solution)/shard_map/all_gather | solution.py:215
  7.9 84.5 %all-gather.7.cloned.1.call-start = ((), (), s32[]{:S(2)}) async-start(), calls=%async_computation.3 | async-start | bytes 2228224 | tf_op jit(solution)/shard_map/all_gather | solution.py:216
  8.7 203.9 %all-gather.9.cloned.1.call-start = ((), (), s32[]{:S(2)}) async-start(), calls=%async_computation.5 | async-start | bytes 4456448 | tf_op jit(solution)/shard_map/all_gather | solution.py:217
  9.4 225.2 %all-gather.11.cloned.1.call-start = ((), (), s32[]{:S(2)}) async-start(), calls=%async_computation.6 | async-start | bytes 4456448 | tf_op jit(solution)/shard_map/all_gather | solution.py:218
  10.0 435.0 %reduce-scatter.3.cloned.1.call-start = ((), (), s32[]{:S(2)}) async-start(), calls=%async_computation.4 | async-start | bytes 4456448 | tf_op jit(solution)/shard_map/reduce_scatter | solution.py:246
  17.0 39.5 %copy-start.7 = (bf16[1,64,1024]{1,2,0:T(8,128)(2,1)}, bf16[1,64,1024]{1,2,0:T(8,128)(2,1)S(1)}, u32[]{:S(2)}) copy-start(bf16[1,64,1024]{1,2,0:T(8,128)(2,1)S(1)} %copy.81) | copy-start | bytes 393220
  17.9 38.6 %copy-start.12 = (f32[32,16]{0,1:T(8,128)S(1)}, f32[32,16]{0,1:T(8,128)}, u32[]{:S(2)}) copy-start(f32[32,16]{0,1:T(8,128)} %param.33) | copy-start | bytes 6148
  106.7 2.5 copy-start.15
  123.8 2.5 copy-start.15
  131.9 12.7 %copy-start.9 = (bf16[64,16,64]{0,2,1:T(8,128)(2,1)}, bf16[64,16,64]{0,2,1:T(8,128)(2,1)S(1)}, u32[]{:S(2)}) copy-start(bf16[64,16,64]{0,2,1:T(8,128)(2,1)S(1)} %get-tuple-element.1967) | copy-start | bytes 393220 | tf_op jit(solution)/shard_map/while
  148.9 1.7 copy-start.3
  168.9 3.3 copy-start.10
  172.3 12.7 %copy-start.9 = (bf16[64,16,64]{0,2,1:T(8,128)(2,1)}, bf16[64,16,64]{0,2,1:T(8,128)(2,1)S(1)}, u32[]{:S(2)}) copy-start(bf16[64,16,64]{0,2,1:T(8,128)(2,1)S(1)} %get-tuple-element.1967) | copy-start | bytes 393220 | tf_op jit(solution)/shard_map/while
  209.2 3.3 copy-start.10
  212.5 6.9 %copy-start.11 = (bf16[64,16,64]{2,0,1:T(8,128)(2,1)S(1)}, bf16[64,16,64]{2,0,1:T(8,128)(2,1)}, u32[]{:S(2)}) copy-start(bf16[64,16,64]{2,0,1:T(8,128)(2,1)} %copy.82) | copy-start | bytes 393220
  212.5 6.8 %copy-start.13 = (f32[16,64]{1,0:T(8,128)S(1)}, f32[16,64]{1,0:T(8,128)}, u32[]{:S(2)}) copy-start(f32[16,64]{1,0:T(8,128)} %custom-call.5) | copy-start | bytes 12292
  212.5 6.8 %copy-start.17 = (f32[16,64]{1,0:T(8,128)S(1)}, f32[16,64]{1,0:T(8,128)}, u32[]{:S(2)}) copy-start(f32[16,64]{1,0:T(8,128)} %custom-call.6) | copy-start | bytes 12292
  212.5 6.8 %copy-start.18 = (s32[2048]{0:T(1024)S(1)}, s32[2048]{0:T(1024)}, u32[]{:S(2)}) copy-start(s32[2048]{0:T(1024)} %convert_reduce_fusion) | copy-start | bytes 24580
  212.5 234.2 %reduce-scatter.5.cloned.1.call-start = ((), (), s32[]{:S(2)}) async-start(), calls=%async_computation.7 | async-start | bytes 8912896 | tf_op jit(solution)/shard_map/reduce_scatter | solution.py:249
  234.6 6.7 %copy-start.14 = (f32[64,16,64]{0,2,1:T(8,128)S(1)}, f32[64,16,64]{0,2,1:T(8,128)}, u32[]{:S(2)}) copy-start(f32[64,16,64]{0,2,1:T(8,128)} %custom-call.7) | copy-start | bytes 786436
  241.3 16.1 %copy-start.1 = (bf16[1,64,1024]{1,2,0:T(8,128)(2,1)S(1)}, bf16[1,64,1024]{1,2,0:T(8,128)(2,1)}, u32[]{:S(2)}) copy-start(bf16[1,64,1024]{1,2,0:T(8,128)(2,1)} %copy.84) | copy-start | bytes 393220
  241.3 16.2 %copy-start.6 = (f32[64,16,64]{0,2,1:T(8,128)S(1)}, f32[64,16,64]{0,2,1:T(8,128)}, u32[]{:S(2)}) copy-start(f32[64,16,64]{0,2,1:T(8,128)} %custom-call.8) | copy-start | bytes 786436
  241.3 16.2 %copy-start.8 = (bf16[1,64,1024]{1,2,0:T(8,128)(2,1)S(1)}, bf16[1,64,1024]{1,2,0:T(8,128)(2,1)}, u32[]{:S(2)}) copy-start(bf16[1,64,1024]{1,2,0:T(8,128)(2,1)} %copy-done.7) | copy-start | bytes 393220
  (16 other events, 22.0 us)
Sparse Core Ops, SparseCore 0:
  9.8 42.6 all-gather.4
  54.4 38.0 all-gather.6
  94.3 40.5 all-gather.8
  136.5 40.8 all-gather.10
  212.6 61.6 reduce-scatter.2
  311.7 69.7 reduce-scatter.4
where the time goes:
time: 458 us; the launch traced here: 455 us
  local copies, waits for them, and re-layouts  170 us (37%)
  blocking collectives  130 us (28%)
  matrix products  67.9 us (15%)
  waiting for transfers between devices  41.4 us (9%)
  other arithmetic  17.8 us (4%)
  between operations  14.5 us (3%)
  loops' own time  13.3 us (3%)
    psum x1, blocking collectives, on_device(): bias_total = lax.psum(self_bias, ('dp', 'seq'))  130 us
    all_gather x1, waiting for transfers between devices, on_device(): lax.all_gather(k_self, 'seq', axis=1, tiled=True)  34.6 us
    dynamic_update_slice x12, local copies, waits for them, and re-layouts, query_side(): lax.scan(grad_step, grad_state, block_ids)  29.1 us
    dot_general x12, matrix products, scores_of(): jnp.einsum('thd,uhd->htu', queries, key_block, preferred_element_type=jnp...  24.8 us
    dot_general x6, matrix products, out_step(): jnp.einsum('htu,uhd->thd', narrow_weights, value_block, preferred_element...  17.1 us
    rev x6, local copies, waits for them, and re-layouts, spread(): return skewed[..., ::-1]  15.1 us
    reshape x6, local copies, waits for them, and re-layouts, spread(): flat_rows = tiled_rows.reshape(leading + (row_count * full_span,))  14.9 us
    reshape x6, local copies, waits for them, and re-layouts, spread(): flat_rows.reshape(leading + (row_count, full_span + 1))[..., :col_count]  14.6 us
  transfers between devices with their start and end apart: 6, of which 2 were waited for; matrix products, arithmetic and copies ran while one was open for 52% of the time, Pallas kernels for 0%

commit v1 on v0

--- a/solution.py
+++ b/solution.py
@@ -253,7 +253,7 @@
     self_value_grad = self_sums[:, feature_count:]
     cross_key_grad = cross_sums[:, :feature_count]
     cross_value_grad = cross_sums[:, feature_count:]
-    bias_total = lax.psum(self_bias, ("dp", "seq"))
+    bias_total = jnp.sum(lax.all_gather(self_bias, ("dp", "seq")), axis=0)
     bias_grad = bias_total * (1.0 / math.sqrt(lax.axis_size("dp") * dec_total))
     return (
         self_dq.reshape(1, dec_rows, feature_count),

time: 458 us -> 393 us (0.86)
  blocking collectives: 130 us -> 49.9 us
  waiting for transfers between devices: 41.4 us -> 56.2 us
    psum x1 -> x0, blocking collectives: 130 us -> none  [on_device(): bias_total = lax.psum(self_bias, ('dp', 'seq'))]
    all_gather x0 -> x1, blocking collectives: none -> 49.9 us  [on_device(): bias_total = jnp.sum(lax.all_gather(self_bias, ('dp', 'seq')), axis=0)]
    reduce_scatter x1, waiting for transfers between devices: 0.01 us -> 14.9 us  [on_device(): lax.psum_scatter(cross_terms.astype(jnp.float32).astype(jnp.bfloat16), 's...]
  transfers between devices with their start and end apart: 6 -> 6, of which waited for: 2 -> 3; matrix products, arithmetic and copies ran while one was open for 52% -> 60% of each run, Pallas kernels for 0% -> 0%
where the time goes in v1:
time: 393 us; the launch traced here: 390 us
  local copies, waits for them, and re-layouts  170 us (43%)
  matrix products  67.9 us (17%)
  waiting for transfers between devices  56.2 us (14%)
  blocking collectives  49.9 us (13%)
  other arithmetic  17.9 us (5%)
  between operations  14.5 us (4%)
  loops' own time  13.3 us (3%)
    all_gather x1, blocking collectives, on_device(): bias_total = jnp.sum(lax.all_gather(self_bias, ('dp', 'seq')), axis=0)  49.9 us
    all_gather x1, waiting for transfers between devices, on_device(): lax.all_gather(k_self, 'seq', axis=1, tiled=True)  34.6 us
    dynamic_update_slice x12, local copies, waits for them, and re-layouts, query_side(): lax.scan(grad_step, grad_state, block_ids)  29.1 us
    dot_general x12, matrix products, scores_of(): jnp.einsum('thd,uhd->htu', queries, key_block, preferred_element_type=jnp...  24.8 us
    dot_general x6, matrix products, out_step(): jnp.einsum('htu,uhd->thd', narrow_weights, value_block, preferred_element...  17.1 us
    rev x6, local copies, waits for them, and re-layouts, spread(): return skewed[..., ::-1]  15.1 us
    reshape x6, local copies, waits for them, and re-layouts, spread(): flat_rows = tiled_rows.reshape(leading + (row_count * full_span,))  14.9 us
    reduce_scatter x1, waiting for transfers between devices, on_device(): lax.psum_scatter(cross_terms.astype(jnp.float32).astype(jnp.bfloat16), 's...  14.9 us
  transfers between devices with their start and end apart: 6, of which 3 were waited for; matrix products, arithmetic and copies ran while one was open for 60% of the time, Pallas kernels for 0%

profile of v1, /device:TPU:2, one launch (start us, length us, event | category | flops | bytes accessed | tf_op | source)
XLA Modules:
  0.0 390.1 jit_solution(10132244589209230313)
XLA Ops:
  17.9 34.6 %all-gather.7.cloned.1.call-done = bf16[1,1024,1024]{2,1,0:T(8,128)(2,1)} async-done(((bf16[1,64,1024]{2,1,0:T(8,128)(2,1)}), bf16[1,1024,1024]{2,1,0:T(8,128)(2,1)}) %all-gather.7.cloned.1.call-update) | async-done | bytes 2097168 | tf_op jit(solution)/shard_map/all_gather | solution.py:215
  52.6 3.9 %copy.92 = bf16[1,1024,1024]{1,2,0:T(8,128)(2,1)} copy(bf16[1,1024,1024]{2,1,0:T(8,128)(2,1)} %all-gather.7.cloned.1.call-done) | data formatting | bytes 4194304 | tf_op jit(solution)/shard_map/all_gather | solution.py:215
  56.5 31.9 %while.91 = (s32[]{:T(128)}, f32[16,64]{1,0:T(8,128)S(1)}, f32[16,64]{1,0:T(8,128)S(1)}, s32[64]{0:T(128)S(1)}, s32[2]{0:T(128)S(1)}, /*index=5*/s32[1024]{0:T(1...) while((s32[]{:T(128)}, f32[16,64]{1,0:T(8,128)S(1)}, ...), condition=%wide.region_5.6_spmd.clone.clone.clone, body=%wide.region_2.0_spmd.clone.clone.clone.sunk | while | flops 73413688 | bytes 34665884 | solution.py:115
  88.4 4.1 %all-gather.9.cloned.1.call-done = bf16[1,1024,1024]{2,1,0:T(8,128)(2,1)} async-done(((bf16[1,64,1024]{2,1,0:T(8,128)(2,1)}), bf16[1,1024,1024]{2,1,0:T(8,128)(2,1)}) %all-gather.9.cloned.1.call-update) | async-done | bytes 2097168 | tf_op jit(solution)/shard_map/all_gather | solution.py:216
  92.5 3.9 %copy.96 = bf16[1,1024,1024]{1,2,0:T(8,128)(2,1)} copy(bf16[1,1024,1024]{2,1,0:T(8,128)(2,1)} %all-gather.9.cloned.1.call-done) | data formatting | bytes 4194304 | tf_op jit(solution)/shard_map/all_gather | solution.py:216
  96.4 34.2 %while.92 = (s32[]{:T(128)}, f32[64,16,64]{0,2,1:T(8,128)}, s32[2]{0:T(128)S(1)}, bf16[1024,16,64]{0,2,1:T(8,128)(2,1)}, s32[64]{0:T(128)S(1)}, /*index=5*/s32[1...) while((s32[]{:T(128)}, f32[64,16,64]{0,2,1:T(8,128)}, ...), condition=%wide.region_7.8_spmd.clone.clone.clone, body=%wide.region_6.7_spmd.clone.clone.clone.sunk | while | flops 140648496 | bytes 34098144 | solution.py:132
  109.2 3.4 fusion.213
  126.3 3.4 fusion.213
  131.7 80.7 %while.93 = (s32[]{:T(128)}, f32[64,16,64]{0,2,1:T(8,128)}, f32[32,16]{0,1:T(8,128)S(1)}, bf16[2,512,2048]{2,1,0:T(8,128)(2,1)}, s32[2]{0:T(128)S(1)}, /*index=5...) while((s32[]{:T(128)}, f32[64,16,64]{0,2,1:T(8,128)}, ...), condition=%wide.region_10.11_spmd.clone.clone.clone, body=%wide.region_8.10_spmd.clone.clone.clone.sunk | while | flops 353446976 | bytes 101543680 | solution.py:179
  164.8 3.7 reshape.730
  168.9 3.3 constant_dynamic-update-slice_fusion.5
  205.1 3.7 reshape.730
  209.2 3.3 constant_dynamic-update-slice_fusion.5
  212.6 6.7 %copy.101 = bf16[1,2048,1024]{1,2,0:T(8,128)(2,1)} copy(bf16[1,2048,1024]{2,1,0:T(8,128)(2,1)} %all-gather.11.cloned.1.call-done) | data formatting | bytes 8388608 | tf_op jit(solution)/shard_map/all_gather | solution.py:217
  219.4 15.2 %while.88 = (s32[]{:T(128)}, f32[16,64]{1,0:T(8,128)S(1)}, f32[16,64]{1,0:T(8,128)S(1)}, s32[64]{0:T(128)S(1)}, s32[4]{0:T(128)S(1)}, /*index=5*/s32[2048]{0:T(1...) while((s32[]{:T(128)}, f32[16,64]{1,0:T(8,128)S(1)}, ...), condition=%wide.region_17.18_spmd.clone, body=%wide.region_14.17_spmd.clone.sunk | while | flops 69768200 | bytes 5532106 | solution.py:115
  234.6 6.6 %copy.105 = bf16[1,2048,1024]{1,2,0:T(8,128)(2,1)} copy(bf16[1,2048,1024]{2,1,0:T(8,128)(2,1)} %all-gather.13.cloned.1.call-done) | data formatting | bytes 8388608 | tf_op jit(solution)/shard_map/all_gather | solution.py:218
  241.3 16.1 %while.89 = (s32[]{:T(128)}, f32[64,16,64]{0,2,1:T(8,128)S(1)}, s32[4]{0:T(128)S(1)}, bf16[2048,16,64]{0,2,1:T(8,128)(2,1)}, s32[64]{0:T(128)S(1)}, /*index=5*/s...) while((s32[]{:T(128)}, f32[64,16,64]{0,2,1:T(8,128)S(1)}, ...), condition=%wide.region_19.20_spmd.clone, body=%wide.region_18.19_spmd.clone.sunk | while | flops 136478720 | bytes 2834388 | solution.py:132
  257.5 54.1 %while.90 = (s32[]{:T(128)}, f32[64,16,64]{0,2,1:T(8,128)S(1)}, bf16[4,512,2048]{2,1,0:T(8,128)(2,1)}, s32[4]{0:T(128)S(1)}, bf16[2048,16,64]{0,2,1:T(8,128)(2,1...) while((s32[]{:T(128)}, f32[64,16,64]{0,2,1:T(8,128)S(1)}, ...), condition=%wide.region_21.22_spmd.clone, body=%wide.region_20.21_spmd.clone.sunk | while | flops 344621056 | bytes 28396028 | solution.py:179
  266.6 2.9 copy.138
  280.2 2.9 copy.138
  293.6 2.9 copy.138
  307.1 2.9 copy.138
  313.4 49.9 %all-gather.1 = f32[64,32,16]{1,2,0:T(8,128)S(1)} all-gather(f32[1,32,16]{1,2,0:T(8,128)S(1)} %bitcast.261), channel_id=2, replica_groups=mesh['dp'=4,'seq'=16,'mp'=4] {'dp','seq'}, dimensions={0}, use_global_device_ids=true | all-gather | bytes 133120 | tf_op jit(solution)/shard_map/all_gather | solution.py:256
  366.5 14.9 %reduce-scatter.5.cloned.1.call-done = bf16[128,2048]{1,0:T(8,128)(2,1)} async-done(((bf16[2048,2048]{1,0:T(8,128)(2,1)}), bf16[128,2048]{1,0:T(8,128)(2,1)}) %reduce-scatter.5.cloned.1.call-update) | async-done | bytes 524304 | tf_op jit(solution)/shard_map/reduce_scatter | solution.py:249
  (319 shorter events, 205.1 us)
Async XLA Ops:
  7.2 9.6 %copy-start.19 = (bf16[1,64,1024]{2,1,0:T(8,128)(2,1)S(1)}, bf16[1,64,1024]{2,1,0:T(8,128)(2,1)}, u32[]{:S(2)}) copy-start(bf16[1,64,1024]{2,1,0:T(8,128)(2,1)} %param.27) | copy-start | bytes 393220
  7.2 45.4 %all-gather.7.cloned.1.call-start = ((), (), s32[]{:S(2)}) async-start(), calls=%async_computation.2 | async-start | bytes 2228224 | tf_op jit(solution)/shard_map/all_gather | solution.py:215
  7.9 84.5 %all-gather.9.cloned.1.call-start = ((), (), s32[]{:S(2)}) async-start(), calls=%async_computation.3 | async-start | bytes 2228224 | tf_op jit(solution)/shard_map/all_gather | solution.py:216
  8.7 203.9 %all-gather.11.cloned.1.call-start = ((), (), s32[]{:S(2)}) async-start(), calls=%async_computation.5 | async-start | bytes 4456448 | tf_op jit(solution)/shard_map/all_gather | solution.py:217
  9.4 225.2 %all-gather.13.cloned.1.call-start = ((), (), s32[]{:S(2)}) async-start(), calls=%async_computation.6 | async-start | bytes 4456448 | tf_op jit(solution)/shard_map/all_gather | solution.py:218
  10.0 354.8 %reduce-scatter.3.cloned.1.call-start = ((), (), s32[]{:S(2)}) async-start(), calls=%async_computation.4 | async-start | bytes 4456448 | tf_op jit(solution)/shard_map/reduce_scatter | solution.py:246
  17.0 39.5 %copy-start.7 = (bf16[1,64,1024]{1,2,0:T(8,128)(2,1)}, bf16[1,64,1024]{1,2,0:T(8,128)(2,1)S(1)}, u32[]{:S(2)}) copy-start(bf16[1,64,1024]{1,2,0:T(8,128)(2,1)S(1)} %copy.103) | copy-start | bytes 393220
  17.9 38.6 %copy-start.12 = (f32[32,16]{0,1:T(8,128)S(1)}, f32[32,16]{0,1:T(8,128)}, u32[]{:S(2)}) copy-start(f32[32,16]{0,1:T(8,128)} %param.33) | copy-start | bytes 6148
  106.7 2.5 copy-start.15
  123.8 2.5 copy-start.15
  131.9 12.7 %copy-start.9 = (bf16[64,16,64]{0,2,1:T(8,128)(2,1)}, bf16[64,16,64]{0,2,1:T(8,128)(2,1)S(1)}, u32[]{:S(2)}) copy-start(bf16[64,16,64]{0,2,1:T(8,128)(2,1)S(1)} %get-tuple-element.2007) | copy-start | bytes 393220 | tf_op jit(solution)/shard_map/while
  148.9 1.7 copy-start.3
  168.9 3.3 copy-start.10
  172.3 12.7 %copy-start.9 = (bf16[64,16,64]{0,2,1:T(8,128)(2,1)}, bf16[64,16,64]{0,2,1:T(8,128)(2,1)S(1)}, u32[]{:S(2)}) copy-start(bf16[64,16,64]{0,2,1:T(8,128)(2,1)S(1)} %get-tuple-element.2007) | copy-start | bytes 393220 | tf_op jit(solution)/shard_map/while
  209.2 3.3 copy-start.10
  212.5 6.9 %copy-start.11 = (bf16[64,16,64]{2,0,1:T(8,128)(2,1)S(1)}, bf16[64,16,64]{2,0,1:T(8,128)(2,1)}, u32[]{:S(2)}) copy-start(bf16[64,16,64]{2,0,1:T(8,128)(2,1)} %copy.104) | copy-start | bytes 393220
  212.5 6.8 %copy-start.13 = (f32[16,64]{1,0:T(8,128)S(1)}, f32[16,64]{1,0:T(8,128)}, u32[]{:S(2)}) copy-start(f32[16,64]{1,0:T(8,128)} %custom-call.5) | copy-start | bytes 12292
  212.5 6.8 %copy-start.17 = (f32[16,64]{1,0:T(8,128)S(1)}, f32[16,64]{1,0:T(8,128)}, u32[]{:S(2)}) copy-start(f32[16,64]{1,0:T(8,128)} %custom-call.6) | copy-start | bytes 12292
  212.5 6.8 %copy-start.18 = (s32[2048]{0:T(1024)S(1)}, s32[2048]{0:T(1024)}, u32[]{:S(2)}) copy-start(s32[2048]{0:T(1024)} %convert_reduce_fusion) | copy-start | bytes 24580
  212.5 168.9 %reduce-scatter.5.cloned.1.call-start = ((), (), s32[]{:S(2)}) async-start(), calls=%async_computation.7 | async-start | bytes 8912896 | tf_op jit(solution)/shard_map/reduce_scatter | solution.py:249
  234.6 6.7 %copy-start.14 = (f32[64,16,64]{0,2,1:T(8,128)S(1)}, f32[64,16,64]{0,2,1:T(8,128)}, u32[]{:S(2)}) copy-start(f32[64,16,64]{0,2,1:T(8,128)} %custom-call.7) | copy-start | bytes 786436
  241.3 16.1 %copy-start.1 = (bf16[1,64,1024]{1,2,0:T(8,128)(2,1)S(1)}, bf16[1,64,1024]{1,2,0:T(8,128)(2,1)}, u32[]{:S(2)}) copy-start(bf16[1,64,1024]{1,2,0:T(8,128)(2,1)} %copy.106) | copy-start | bytes 393220
  241.3 16.2 %copy-start.6 = (f32[64,16,64]{0,2,1:T(8,128)S(1)}, f32[64,16,64]{0,2,1:T(8,128)}, u32[]{:S(2)}) copy-start(f32[64,16,64]{0,2,1:T(8,128)} %custom-call.8) | copy-start | bytes 786436
  241.3 16.2 %copy-start.8 = (bf16[1,64,1024]{1,2,0:T(8,128)(2,1)S(1)}, bf16[1,64,1024]{1,2,0:T(8,128)(2,1)}, u32[]{:S(2)}) copy-start(bf16[1,64,1024]{1,2,0:T(8,128)(2,1)} %copy-done.7) | copy-start | bytes 393220
  (16 other events, 22.0 us)
Sparse Core Ops, SparseCore 0:
  9.8 42.6 all-gather.6
  54.4 38.0 all-gather.8
  94.3 40.5 all-gather.10
  136.5 40.8 all-gather.12
  212.6 61.6 reduce-scatter.2
  311.7 69.6 reduce-scatter.4
